TPU v7x, 32 devices: a whole 2x2x4 slice. The times are simulated.
32 devices in a mesh: grp: 4 (over y, x), dev: 8 (over z, core).
Axes of the slice: x: 2, y: 2, z: 4, core: 2. Of those that a mesh axis runs over, the one named last changes fastest.
Arguments:
- points: float32 [64, 49152], P(None, 'dev'), may hold values from -6 to 6
- weights: float32 [49152, 128], P('dev'), may hold values from -4 to 4
- proj: float32 [256, 49152], P(None, 'dev'), may hold values from -0.078125 to 0.078125
- fetch_table: int32 [3, 8, 8, 2], P(None, 'dev'), may hold values from 0 to 11, as said below
- near_list: int32 [96, 16], P('dev'), may hold values from 0 to 15, as said below
- far_list: int32 [96, 8], P('dev'), may hold values from 0 to 7, as said below
- skel_idx: int32 [8, 256], P('dev'), may hold values from 0 to 6143, as said below
Outputs:
- potential: float32 [49152, 128], P('dev')
Inputs may be any that keep to these rules, and one draw needn't show every extreme that they name: Entries of fetch_table[r, d, e] are distinct local leaf numbers of column e. `near_list`: the 16 slots of one target leaf are distinct. `far_list`: the 8 nodes of one target leaf are distinct, and one of them is node (c + 1) mod 8 for the leaf's column c. `skel_idx`: the 256 skeleton points of one node are distinct.
All inputs are finite; a program needn't handle non-finite values.
Results may differ from a plain program's by a relative error of at most 0.0003.
Values sent between devices are 32-bit elements; how exact they have to be, the bound alone decides.
No kernel may reach another device: no remote copies, remote signals or barrier semaphores. Data moves between devices by JAX's collectives and lax.ppermute only.
A program may use at most 192 MiB of HBM per device.

v0:
```python
import jax
import jax.numpy as jnp
from jax import lax
from jax.sharding import PartitionSpec as P


def kernel_sum(target, sources, values):
    high = lax.Precision.HIGHEST
    inner = jnp.einsum("dt,jds->tjs", target, sources, precision=high)
    target_norm = jnp.sum(target * target, axis=0)
    source_norm = jnp.sum(sources * sources, axis=1)
    distance = target_norm[:, None, None] + source_norm[None] - 2.0 * inner
    kernel = jnp.exp(-distance * (2.0 / target.shape[0]))
    return jnp.einsum("tjs,jsw->tw", kernel, values, precision=high)


def on_device(points, weights, proj, fetch_table, near_list, far_list, skel_idx):
    features, column_points = points.shape
    columns = weights.shape[1]
    devices = lax.axis_size("dev")
    groups = lax.axis_size("grp")
    targets = near_list.shape[0]
    leaf_size = column_points // targets
    row_leaves = targets // (groups - 1)
    capacity = fetch_table.shape[3]
    group_index = lax.axis_index("grp")
    near_row = jnp.minimum(group_index, groups - 2)
    far_side = group_index == groups - 1
    leaf_coords = points.reshape(features, targets, leaf_size)
    leaf_weights = weights.reshape(targets, leaf_size, columns)
    requests = lax.dynamic_index_in_dim(fetch_table[:, 0], near_row, 0, keepdims=False)
    asked = lax.all_to_all(requests, "dev", split_axis=0, concat_axis=0, tiled=True)
    coords = jnp.moveaxis(jnp.take(leaf_coords, asked, axis=1), 0, 2)
    values = jnp.take(leaf_weights, asked, axis=0)
    fetched_coords = lax.all_to_all(coords, "dev", split_axis=0, concat_axis=0, tiled=True)
    fetched_values = lax.all_to_all(values, "dev", split_axis=0, concat_axis=0, tiled=True)
    flat_coords = fetched_coords.reshape(devices * capacity, features, leaf_size)
    flat_values = fetched_values.reshape(devices * capacity, leaf_size, columns)
    local_skeleton = jnp.take(points, skel_idx[0], axis=1)
    share_len = column_points // groups
    share_start = group_index * share_len
    share_proj = lax.dynamic_slice_in_dim(proj, share_start, share_len, 1)
    share_weights = lax.dynamic_slice_in_dim(weights, share_start, share_len, 0)
    partial_value = jnp.dot(
        share_proj,
        share_weights,
        preferred_element_type=jnp.float32,
        precision=lax.Precision.HIGHEST,
    )
    node_weights = lax.psum(partial_value, "grp")
    skel_coords, skel_weights = (
        lax.all_gather(local_skeleton[None], "dev", axis=0, tiled=True),
        lax.all_gather(node_weights[None], "dev", axis=0, tiled=True),
    )

    def near_work():
        slots = lax.dynamic_slice_in_dim(near_list, near_row * row_leaves, row_leaves, 0)
        leaf_numbers = near_row * row_leaves + jnp.arange(row_leaves, dtype=jnp.int32)

        def near_leaf(items):
            leaf_number, leaf_slots = items
            target = jnp.take(leaf_coords, leaf_number, axis=1)
            return kernel_sum(
                target,
                jnp.take(flat_coords, leaf_slots, axis=0),
                jnp.take(flat_values, leaf_slots, axis=0),
            )

        block = lax.map(near_leaf, (leaf_numbers, slots))
        empty = jnp.zeros((targets, leaf_size, columns), jnp.float32)
        return lax.dynamic_update_slice_in_dim(empty, block, near_row * row_leaves, 0)

    def far_work():

        def far_leaf(items):
            leaf_number, node_ids = items
            target = jnp.take(leaf_coords, leaf_number, axis=1)
            return kernel_sum(
                target,
                jnp.take(skel_coords, node_ids, axis=0),
                jnp.take(skel_weights, node_ids, axis=0),
            )

        return lax.map(far_leaf, (jnp.arange(targets, dtype=jnp.int32), far_list))

    contribution = lax.cond(far_side, far_work, near_work)
    total = lax.psum(contribution, "grp")
    return total.reshape(column_points, columns)


def solution(mesh):
    placed = (
        P(None, "dev"),
        P("dev", None),
        P(None, "dev"),
        P(None, "dev", None, None),
        P("dev", None),
        P("dev", None),
        P("dev", None),
    )
    return jax.shard_map(
        on_device, mesh=mesh, in_specs=placed, out_specs=P("dev", None), check_vma=False
    )
```

profile of v0, /device:TPU:0, one launch (start us, length us, event | category | flops | bytes accessed | tf_op | source)
XLA Modules:
  0.0 515.7 jit_solution(13828682134783458848)
XLA Ops:
  8.0 6.4 %all-to-all-start = ((s32[8,1,2]{2,1,0:T(1,128)}), s32[8,1,2]{2,1,0:T(1,128)S(1)}, u32[]{:S(2)}, u32[]{:S(2)}) async-start(s32[8,1,2]{2,1,0:T(1,128)} %copy.24), calls=%async_computation | async-start | bytes 8192 | tf_op jit(solution)/shard_map/all_to_all | solution.py:32
  14.4 2.7 copy.52
  17.1 2.8 all-to-all-done
  20.3 3.4 gather_fusion.4
  23.7 3.3 broadcast_select_fusion.1
  27.0 4.4 all-to-all-start.1
  31.4 2.8 gather_fusion.5
  34.2 4.6 broadcast_select_fusion
  38.8 41.6 %all-to-all-done.1 = f32[8,2,64,512]{3,2,1,0:T(8,128)} async-done(((f32[8,2,64,512]{3,2,1,0:T(8,128)}), f32[8,2,64,512]{3,2,1,0:T(8,128)}, u32[]{:S(2)}, u32[]{:S(2)}) %all-to-all-start.1) | async-done | bytes 2097184 | tf_op jit(solution)/shard_map/all_to_all | solution.py:35
  80.4 4.6 all-to-all-start.2
  85.0 3.5 fusion.72
  88.6 43.7 %all-reduce.3.cloned.1.call-done = f32[1,256,128]{2,1,0:T(8,128)} async-done(((f32[1,256,128]{2,1,0:T(8,128)}), f32[1,256,128]{2,1,0:T(8,128)}) %all-reduce.3.cloned.1.call-update) | async-done | bytes 131088 | tf_op jit(solution)/shard_map/psum | solution.py:50
  132.4 2.9 reshape.190
  137.5 2.6 gather_fusion.6
  140.3 56.1 %all_gather.6 = f32[8,64,256]{2,1,0:T(8,128)} all-gather(f32[1,64,256]{2,1,0:T(8,128)S(1)} %copy.32), channel_id=1, replica_groups=mesh['grp'=4,'dev'=8] {'dev'}, dimensions={0}, use_global_device_ids=true | all-gather | bytes 589824 | tf_op jit(solution)/shard_map/all_gather | solution.py:52
  196.5 202.2 %conditional.1 = (f32[12,512,128]{2,1,0:T(8,128)}) conditional(s32[]{:T(128)} %convert_element_type.3, (s32[]{:T(128)}, s32[12,16]{1,0:T(8,128)}, f32[8,2,64,512]{3,2,1,0:T(8,128)}, f32[8,2,512,128]{3,2,1,0:T(8,128)}, f32[64,12,512]{2,1,0:T(8,128)}) %tuple.20, (f32[64,12,512]{2,1,0:T(8,128)}, s32[12,8]{0,1:T(8,128)S(1)}, f32[8,64,256]{2,1,0:T(8,128)}, ...), branch_computations={%region_1.7_spmd, %region_6.12_spmd} | conditional | flops 9687917568 | bytes 60630836 | solution.py:86
  197.2 197.3 %while.19 = (s32[]{:T(128)}, f32[4,512,128]{2,1,0:T(8,128)}, s32[4]{0:T(128)S(1)}, f32[64,12,512]{2,1,0:T(8,128)}, s32[4,16]{1,0:T(4,128)S(1)}, /*index=5*/f32[1...) while((s32[]{:T(128)}, f32[4,512,128]{2,1,0:T(8,128)}, ...), condition=%wide.region_5.6_spmd, body=%wide.region_2.5_spmd.sunk | while | flops 9687917568 | bytes 55387260 | solution.py:69
  201.1 2.3 gather_fusion.3
  203.4 16.2 %fusion.106 = f32[512,16,512]{2,0,1:T(8,128)} fusion(f32[16,64,512]{2,1,0:T(8,128)S(1)} %gather_fusion.3, pred[16]{0:T(512)(128)(4,1)S(1)} %compare_and_fusion.7, f32[64,1,512]{2,1,0:T(1,128)S(1)} %constant_dynamic-slice_fusion.8, pred[]{:T(512)S(6)} %and.56), kind=kOutput, calls=%fused_computation.22.clone.1 | convolution fusion | flops 3221782528 | bytes 19005456 | tf_op jit(solution)/shard_map/cond/branch_0_fun/while/body/eval_jaxpr/dt,jds->tjs/dot_general | solution.py:9
  220.0 5.0 gather_fusion.2
  225.0 21.5 %fusion.108 = f32[4,512,128]{2,1,0:T(8,128)} fusion(f32[4,512,128]{2,1,0:T(8,128)} %get-tuple-element.303, s32[]{:T(128)} %get-tuple-element.302, f32[16,512,128]{2,1,0:T(8,128)} %gather_fusion.2, pred[16]{0:T(512)(128)(4,1)S(1)} %compare_and_fusion.7, f32[512,16,512]{2,0,1:T(8,128)} %fusion.106, f32[16,512]{1,0:T(8,128)S(1)} %multiply_reduce_fusion.5, ...), kind=kOutput, calls=%fused_computation.25.clone.1 | convolution fusion | flops 6464471040 | bytes 21269008 | tf_op jit(solution)/shard_map/cond/branch_0_fun/while/body/eval_jaxpr/tjs,jsw->tw/dot_general | solution.py:14
  252.7 16.2 %fusion.106 = f32[512,16,512]{2,0,1:T(8,128)} fusion(f32[16,64,512]{2,1,0:T(8,128)S(1)} %gather_fusion.3, pred[16]{0:T(512)(128)(4,1)S(1)} %compare_and_fusion.7, f32[64,1,512]{2,1,0:T(1,128)S(1)} %constant_dynamic-slice_fusion.8, pred[]{:T(512)S(6)} %and.56), kind=kOutput, calls=%fused_computation.22.clone.1 | convolution fusion | flops 3221782528 | bytes 19005456 | tf_op jit(solution)/shard_map/cond/branch_0_fun/while/body/eval_jaxpr/dt,jds->tjs/dot_general | solution.py:9
  269.3 5.0 gather_fusion.2
  274.3 21.5 %fusion.108 = f32[4,512,128]{2,1,0:T(8,128)} fusion(f32[4,512,128]{2,1,0:T(8,128)} %get-tuple-element.303, s32[]{:T(128)} %get-tuple-element.302, f32[16,512,128]{2,1,0:T(8,128)} %gather_fusion.2, pred[16]{0:T(512)(128)(4,1)S(1)} %compare_and_fusion.7, f32[512,16,512]{2,0,1:T(8,128)} %fusion.106, f32[16,512]{1,0:T(8,128)S(1)} %multiply_reduce_fusion.5, ...), kind=kOutput, calls=%fused_computation.25.clone.1 | convolution fusion | flops 6464471040 | bytes 21269008 | tf_op jit(solution)/shard_map/cond/branch_0_fun/while/body/eval_jaxpr/tjs,jsw->tw/dot_general | solution.py:14
  302.1 16.2 %fusion.106 = f32[512,16,512]{2,0,1:T(8,128)} fusion(f32[16,64,512]{2,1,0:T(8,128)S(1)} %gather_fusion.3, pred[16]{0:T(512)(128)(4,1)S(1)} %compare_and_fusion.7, f32[64,1,512]{2,1,0:T(1,128)S(1)} %constant_dynamic-slice_fusion.8, pred[]{:T(512)S(6)} %and.56), kind=kOutput, calls=%fused_computation.22.clone.1 | convolution fusion | flops 3221782528 | bytes 19005456 | tf_op jit(solution)/shard_map/cond/branch_0_fun/while/body/eval_jaxpr/dt,jds->tjs/dot_general | solution.py:9
  318.6 5.0 gather_fusion.2
  323.6 21.5 %fusion.108 = f32[4,512,128]{2,1,0:T(8,128)} fusion(f32[4,512,128]{2,1,0:T(8,128)} %get-tuple-element.303, s32[]{:T(128)} %get-tuple-element.302, f32[16,512,128]{2,1,0:T(8,128)} %gather_fusion.2, pred[16]{0:T(512)(128)(4,1)S(1)} %compare_and_fusion.7, f32[512,16,512]{2,0,1:T(8,128)} %fusion.106, f32[16,512]{1,0:T(8,128)S(1)} %multiply_reduce_fusion.5, ...), kind=kOutput, calls=%fused_computation.25.clone.1 | convolution fusion | flops 6464471040 | bytes 21269008 | tf_op jit(solution)/shard_map/cond/branch_0_fun/while/body/eval_jaxpr/tjs,jsw->tw/dot_general | solution.py:14
  351.4 16.2 %fusion.106 = f32[512,16,512]{2,0,1:T(8,128)} fusion(f32[16,64,512]{2,1,0:T(8,128)S(1)} %gather_fusion.3, pred[16]{0:T(512)(128)(4,1)S(1)} %compare_and_fusion.7, f32[64,1,512]{2,1,0:T(1,128)S(1)} %constant_dynamic-slice_fusion.8, pred[]{:T(512)S(6)} %and.56), kind=kOutput, calls=%fused_computation.22.clone.1 | convolution fusion | flops 3221782528 | bytes 19005456 | tf_op jit(solution)/shard_map/cond/branch_0_fun/while/body/eval_jaxpr/dt,jds->tjs/dot_general | solution.py:9
  367.9 5.0 gather_fusion.2
  372.9 21.5 %fusion.108 = f32[4,512,128]{2,1,0:T(8,128)} fusion(f32[4,512,128]{2,1,0:T(8,128)} %get-tuple-element.303, s32[]{:T(128)} %get-tuple-element.302, f32[16,512,128]{2,1,0:T(8,128)} %gather_fusion.2, pred[16]{0:T(512)(128)(4,1)S(1)} %compare_and_fusion.7, f32[512,16,512]{2,0,1:T(8,128)} %fusion.106, f32[16,512]{1,0:T(8,128)S(1)} %multiply_reduce_fusion.5, ...), kind=kOutput, calls=%fused_computation.25.clone.1 | convolution fusion | flops 6464471040 | bytes 21269008 | tf_op jit(solution)/shard_map/cond/branch_0_fun/while/body/eval_jaxpr/tjs,jsw->tw/dot_general | solution.py:14
  398.7 106.7 %all-reduce.5.cloned.1.call-done = f32[6144,128]{1,0:T(8,128)} async-done(((f32[6144,128]{1,0:T(8,128)}), f32[6144,128]{1,0:T(8,128)}) %all-reduce.5.cloned.1.call-update) | async-done | bytes 3145744 | tf_op jit(solution)/shard_map/psum | solution.py:87
  505.4 3.8 copy.80
  (69 shorter events, 26.0 us)
Async XLA Ops:
  6.5 24.8 %copy-start = (f32[6144,128]{1,0:T(8,128)S(1)}, f32[6144,128]{1,0:T(8,128)}, u32[]{:S(2)}) copy-start(f32[6144,128]{1,0:T(8,128)} %param.16) | copy-start | bytes 9437188
  8.0 11.9 %all-to-all-start = ((s32[8,1,2]{2,1,0:T(1,128)}), s32[8,1,2]{2,1,0:T(1,128)S(1)}, u32[]{:S(2)}, u32[]{:S(2)}) async-start(s32[8,1,2]{2,1,0:T(1,128)} %copy.24), calls=%async_computation | async-start | bytes 8192 | tf_op jit(solution)/shard_map/all_to_all | solution.py:32
  27.0 53.4 %all-to-all-start.1 = ((f32[8,2,64,512]{3,2,1,0:T(8,128)}), f32[8,2,64,512]{3,2,1,0:T(8,128)}, u32[]{:S(2)}, u32[]{:S(2)}) async-start(f32[8,2,64,512]{3,2,1,0:T(8,128)} %broadcast_select_fusion.1), calls=%async_computation.1 | async-start | bytes 4194304 | tf_op jit(solution)/shard_map/all_to_all | solution.py:35
  80.4 116.1 %all-to-all-start.2 = ((f32[8,2,512,128]{3,2,1,0:T(8,128)}), f32[8,2,512,128]{3,2,1,0:T(8,128)}, u32[]{:S(2)}, u32[]{:S(2)}) async-start(f32[8,2,512,128]{3,2,1,0:T(8,128)} %broadcast_select_fusion), calls=%async_computation.2 | async-start | bytes 8388608 | tf_op jit(solution)/shard_map/all_to_all | solution.py:36
  85.0 47.3 %all-reduce.3.cloned.1.call-start = ((), (), s32[]{:S(2)}) async-start(), calls=%async_computation.3 | async-start | bytes 262144 | tf_op jit(solution)/shard_map/psum | solution.py:50
  88.5 46.7 %copy-start.3 = (f32[64,6144]{1,0:T(8,128)S(1)}, f32[64,6144]{1,0:T(8,128)}, u32[]{:S(2)}) copy-start(f32[64,6144]{1,0:T(8,128)} %param.15) | copy-start | bytes 4718596
  88.5 107.9 %all-gather.2.cloned.1.call-start = ((), (), s32[]{:S(2)}) async-start(), calls=%async_computation.4 | async-start | bytes 1179648 | tf_op jit(solution)/shard_map/all_gather | solution.py:53
  132.3 5.2 %copy-start.5 = (s32[1,256]{1,0:T(1,128)S(1)}, s32[1,256]{1,0:T(1,128)}, u32[]{:S(2)}) copy-start(s32[1,256]{1,0:T(1,128)} %param.21) | copy-start | bytes 3076
  132.3 64.1 %copy-start.4 = (s32[12,8]{0,1:T(8,128)S(1)}, s32[12,8]{0,1:T(8,128)}, u32[]{:S(2)}) copy-start(s32[12,8]{0,1:T(8,128)} %param.20) | copy-start | bytes 1156
  132.3 373.1 %all-reduce.5.cloned.1.call-start = ((), (), s32[]{:S(2)}) async-start(), calls=%async_computation.5 | async-start | bytes 6291456 | tf_op jit(solution)/shard_map/psum | solution.py:87
  398.7 110.5 %copy-start.1 = (f32[6144,128]{1,0:T(8,128)S(1)}, f32[6144,128]{1,0:T(8,128)}, u32[]{:S(2)}) copy-start(f32[6144,128]{1,0:T(8,128)} %param.16) | copy-start | bytes 9437188
Sparse Core Ops, SparseCore 0:
  88.7 43.5 all-reduce.2
  133.9 39.0 all-gather.1
  398.8 106.5 all-reduce.4
where the time goes:
time: 518 us; the launch traced here: 516 us
  waiting for transfers between devices  195 us (38%)
  matrix products  154 us (30%)
  local copies, waits for them, and re-layouts  64.2 us (12%)
  blocking collectives  56.1 us (11%)
  starting transfers between devices  15.4 us (3%)
  between operations  13.2 us (3%)
  other arithmetic  9.78 us (2%)
  loops' own time  7.83 us (2%)
    psum x1, waiting for transfers between devices, on_device(): total = lax.psum(contribution, 'grp')  107 us
    dot_general x4, matrix products, kernel_sum(): return jnp.einsum('tjs,jsw->tw', kernel, values, precision=high)  86.1 us
    dot_general x4, matrix products, kernel_sum(): inner = jnp.einsum('dt,jds->tjs', target, sources, precision=high)  64.6 us
    all_gather x1, blocking collectives, on_device(): lax.all_gather(local_skeleton[None], 'dev', axis=0, tiled=True)  56.1 us
    psum x1, waiting for transfers between devices, on_device(): node_weights = lax.psum(partial_value, 'grp')  43.7 us
    all_to_all x1, waiting for transfers between devices, on_device(): lax.all_to_all(coords, 'dev', split_axis=0, concat_axis=0, tiled=True)  41.6 us
    gather x4, local copies, waits for them, and re-layouts, near_leaf(): jnp.take(flat_values, leaf_slots, axis=0)  19.9 us
  transfers between devices with their start and end apart: 6, of which 4 were waited for; matrix products, arithmetic and copies ran while one was open for 4% of the time, Pallas kernels for 0%

commit v1 on v0

--- a/solution.py
+++ b/solution.py
@@ -47,7 +47,11 @@
         preferred_element_type=jnp.float32,
         precision=lax.Precision.HIGHEST,
     )
-    node_weights = lax.psum(partial_value, "grp")
+    node_weights = partial_value
+    for hop in (1, 2):
+        node_weights = node_weights + lax.ppermute(
+            node_weights, "grp", [(dev, dev ^ hop) for dev in range(4)]
+        )
     skel_coords, skel_weights = (
         lax.all_gather(local_skeleton[None], "dev", axis=0, tiled=True),
         lax.all_gather(node_weights[None], "dev", axis=0, tiled=True),

time: 518 us -> 521 us (level)
  blocking collectives: 56.1 us -> 89 us
  waiting for transfers between devices: 195 us -> 163 us
    psum x1 -> x0, waiting for transfers between devices: 43.7 us -> none  [on_device(): node_weights = lax.psum(partial_value, 'grp')]
    all_gather x1, blocking collectives: 56.1 us -> 89 us  [on_device(): lax.all_gather(local_skeleton[None], 'dev', axis=0, tiled=True)]
    ppermute x0 -> x2, waiting for transfers between devices: none -> 7.67 us  [on_device(): lax.ppermute(node_weights, 'grp', [(dev, dev ^ hop) for dev in range(4)])]
  transfers between devices with their start and end apart: 6 -> 7, of which waited for: 4 -> 5; matrix products, arithmetic and copies ran while one was open for 4% -> 4% of each run, Pallas kernels for 0% -> 0%
where the time goes in v1:
time: 521 us; the launch traced here: 519 us
  waiting for transfers between devices  163 us (31%)
  matrix products  154 us (30%)
  blocking collectives  89 us (17%)
  local copies, waits for them, and re-layouts  63.8 us (12%)
  starting transfers between devices  18.5 us (4%)
  between operations  13.5 us (3%)
  other arithmetic  10.5 us (2%)
  loops' own time  7.05 us (1%)
    psum x1, waiting for transfers between devices, on_device(): total = lax.psum(contribution, 'grp')  111 us
    all_gather x1, blocking collectives, on_device(): lax.all_gather(local_skeleton[None], 'dev', axis=0, tiled=True)  89 us
    dot_general x4, matrix products, kernel_sum(): return jnp.einsum('tjs,jsw->tw', kernel, values, precision=high)  86.1 us
    dot_general x4, matrix products, kernel_sum(): inner = jnp.einsum('dt,jds->tjs', target, sources, precision=high)  64.6 us
    all_to_all x1, waiting for transfers between devices, on_device(): lax.all_to_all(coords, 'dev', split_axis=0, concat_axis=0, tiled=True)  41.6 us
    gather x4, local copies, waits for them, and re-layouts, near_leaf(): jnp.take(flat_values, leaf_slots, axis=0)  19.9 us
  transfers between devices with their start and end apart: 7, of which 5 were waited for; matrix products, arithmetic and copies ran while one was open for 4% of the time, Pallas kernels for 0%

profile of v1, /device:TPU:0, one launch (start us, length us, event | category | flops | bytes accessed | tf_op | source)
XLA Modules:
  0.0 518.9 jit_solution(11640831129942706588)
XLA Ops:
  8.0 6.4 %all-to-all-start = ((s32[8,1,2]{2,1,0:T(1,128)}), s32[8,1,2]{2,1,0:T(1,128)S(1)}, u32[]{:S(2)}, u32[]{:S(2)}) async-start(s32[8,1,2]{2,1,0:T(1,128)} %copy.24), calls=%async_computation | async-start | bytes 8192 | tf_op jit(solution)/shard_map/all_to_all | solution.py:32
  14.4 2.7 copy.52
  17.1 2.8 all-to-all-done
  20.3 3.4 gather_fusion.4
  23.7 3.3 broadcast_select_fusion.1
  27.0 4.4 all-to-all-start.1
  31.4 2.8 gather_fusion.5
  34.2 4.6 broadcast_select_fusion
  38.8 41.6 %all-to-all-done.1 = f32[8,2,64,512]{3,2,1,0:T(8,128)} async-done(((f32[8,2,64,512]{3,2,1,0:T(8,128)}), f32[8,2,64,512]{3,2,1,0:T(8,128)}, u32[]{:S(2)}, u32[]{:S(2)}) %all-to-all-start.1) | async-done | bytes 2097184 | tf_op jit(solution)/shard_map/all_to_all | solution.py:35
  80.4 4.6 all-to-all-start.2
  85.0 2.8 fusion.70
  89.4 4.2 collective-permute-done
  95.2 3.4 collective-permute-done.1
  99.5 2.9 reshape.190
  104.6 2.6 gather_fusion.6
  107.4 89.0 %all_gather.6 = f32[8,64,256]{2,1,0:T(8,128)} all-gather(f32[1,64,256]{2,1,0:T(8,128)S(1)} %copy.32), channel_id=1, replica_groups=mesh['grp'=4,'dev'=8] {'dev'}, dimensions={0}, use_global_device_ids=true | all-gather | bytes 589824 | tf_op jit(solution)/shard_map/all_gather | solution.py:56
  196.5 201.0 %conditional.1 = (f32[12,512,128]{2,1,0:T(8,128)}) conditional(s32[]{:T(128)} %convert_element_type.3, (s32[]{:T(128)}, s32[12,16]{1,0:T(8,128)}, f32[8,2,64,512]{3,2,1,0:T(8,128)}, f32[8,2,512,128]{3,2,1,0:T(8,128)}, f32[64,12,512]{2,1,0:T(8,128)}) %tuple.20, (f32[64,12,512]{2,1,0:T(8,128)}, s32[12,8]{0,1:T(8,128)S(1)}, f32[8,64,256]{2,1,0:T(8,128)}, ...), branch_computations={%region_0.6_spmd, %region_5.11_spmd} | conditional | flops 9687917568 | bytes 60630836 | solution.py:90
  197.2 196.1 %while.19 = (s32[]{:T(128)}, f32[4,512,128]{2,1,0:T(8,128)}, s32[4]{0:T(128)S(1)}, f32[64,12,512]{2,1,0:T(8,128)}, s32[4,16]{1,0:T(4,128)S(1)}, /*index=5*/f32[1...) while((s32[]{:T(128)}, f32[4,512,128]{2,1,0:T(8,128)}, ...), condition=%wide.region_4.5_spmd, body=%wide.region_1.4_spmd.sunk | while | flops 9687917568 | bytes 55387260 | solution.py:73
  203.1 16.2 %fusion.103 = f32[512,16,512]{2,0,1:T(8,128)} fusion(f32[16,64,512]{2,1,0:T(8,128)S(1)} %gather_fusion.3, pred[16]{0:T(512)(128)(4,1)S(1)} %compare_and_fusion.7, f32[64,1,512]{2,1,0:T(1,128)S(1)} %constant_dynamic-slice_fusion.8, pred[]{:T(512)S(6)} %and.56), kind=kOutput, calls=%fused_computation.22.clone.1 | convolution fusion | flops 3221782528 | bytes 19005456 | tf_op jit(solution)/shard_map/cond/branch_0_fun/while/body/eval_jaxpr/dt,jds->tjs/dot_general | solution.py:9
  219.7 5.0 gather_fusion.2
  224.7 21.5 %fusion.105 = f32[4,512,128]{2,1,0:T(8,128)} fusion(f32[4,512,128]{2,1,0:T(8,128)} %get-tuple-element.303, s32[]{:T(128)} %get-tuple-element.302, f32[16,512,128]{2,1,0:T(8,128)} %gather_fusion.2, pred[16]{0:T(512)(128)(4,1)S(1)} %compare_and_fusion.7, f32[512,16,512]{2,0,1:T(8,128)} %fusion.103, f32[16,512]{1,0:T(8,128)S(1)} %multiply_reduce_fusion.5, ...), kind=kOutput, calls=%fused_computation.25.clone.1 | convolution fusion | flops 6464471040 | bytes 21269008 | tf_op jit(solution)/shard_map/cond/branch_0_fun/while/body/eval_jaxpr/tjs,jsw->tw/dot_general | solution.py:14
  252.1 16.2 %fusion.103 = f32[512,16,512]{2,0,1:T(8,128)} fusion(f32[16,64,512]{2,1,0:T(8,128)S(1)} %gather_fusion.3, pred[16]{0:T(512)(128)(4,1)S(1)} %compare_and_fusion.7, f32[64,1,512]{2,1,0:T(1,128)S(1)} %constant_dynamic-slice_fusion.8, pred[]{:T(512)S(6)} %and.56), kind=kOutput, calls=%fused_computation.22.clone.1 | convolution fusion | flops 3221782528 | bytes 19005456 | tf_op jit(solution)/shard_map/cond/branch_0_fun/while/body/eval_jaxpr/dt,jds->tjs/dot_general | solution.py:9
  268.7 5.0 gather_fusion.2
  273.7 21.5 %fusion.105 = f32[4,512,128]{2,1,0:T(8,128)} fusion(f32[4,512,128]{2,1,0:T(8,128)} %get-tuple-element.303, s32[]{:T(128)} %get-tuple-element.302, f32[16,512,128]{2,1,0:T(8,128)} %gather_fusion.2, pred[16]{0:T(512)(128)(4,1)S(1)} %compare_and_fusion.7, f32[512,16,512]{2,0,1:T(8,128)} %fusion.103, f32[16,512]{1,0:T(8,128)S(1)} %multiply_reduce_fusion.5, ...), kind=kOutput, calls=%fused_computation.25.clone.1 | convolution fusion | flops 6464471040 | bytes 21269008 | tf_op jit(solution)/shard_map/cond/branch_0_fun/while/body/eval_jaxpr/tjs,jsw->tw/dot_general | solution.py:14
  301.2 16.2 %fusion.103 = f32[512,16,512]{2,0,1:T(8,128)} fusion(f32[16,64,512]{2,1,0:T(8,128)S(1)} %gather_fusion.3, pred[16]{0:T(512)(128)(4,1)S(1)} %compare_and_fusion.7, f32[64,1,512]{2,1,0:T(1,128)S(1)} %constant_dynamic-slice_fusion.8, pred[]{:T(512)S(6)} %and.56), kind=kOutput, calls=%fused_computation.22.clone.1 | convolution fusion | flops 3221782528 | bytes 19005456 | tf_op jit(solution)/shard_map/cond/branch_0_fun/while/body/eval_jaxpr/dt,jds->tjs/dot_general | solution.py:9
  317.7 5.0 gather_fusion.2
  322.7 21.5 %fusion.105 = f32[4,512,128]{2,1,0:T(8,128)} fusion(f32[4,512,128]{2,1,0:T(8,128)} %get-tuple-element.303, s32[]{:T(128)} %get-tuple-element.302, f32[16,512,128]{2,1,0:T(8,128)} %gather_fusion.2, pred[16]{0:T(512)(128)(4,1)S(1)} %compare_and_fusion.7, f32[512,16,512]{2,0,1:T(8,128)} %fusion.103, f32[16,512]{1,0:T(8,128)S(1)} %multiply_reduce_fusion.5, ...), kind=kOutput, calls=%fused_computation.25.clone.1 | convolution fusion | flops 6464471040 | bytes 21269008 | tf_op jit(solution)/shard_map/cond/branch_0_fun/while/body/eval_jaxpr/tjs,jsw->tw/dot_general | solution.py:14
  350.2 16.2 %fusion.103 = f32[512,16,512]{2,0,1:T(8,128)} fusion(f32[16,64,512]{2,1,0:T(8,128)S(1)} %gather_fusion.3, pred[16]{0:T(512)(128)(4,1)S(1)} %compare_and_fusion.7, f32[64,1,512]{2,1,0:T(1,128)S(1)} %constant_dynamic-slice_fusion.8, pred[]{:T(512)S(6)} %and.56), kind=kOutput, calls=%fused_computation.22.clone.1 | convolution fusion | flops 3221782528 | bytes 19005456 | tf_op jit(solution)/shard_map/cond/branch_0_fun/while/body/eval_jaxpr/dt,jds->tjs/dot_general | solution.py:9
  366.8 5.0 gather_fusion.2
  371.7 21.5 %fusion.105 = f32[4,512,128]{2,1,0:T(8,128)} fusion(f32[4,512,128]{2,1,0:T(8,128)} %get-tuple-element.303, s32[]{:T(128)} %get-tuple-element.302, f32[16,512,128]{2,1,0:T(8,128)} %gather_fusion.2, pred[16]{0:T(512)(128)(4,1)S(1)} %compare_and_fusion.7, f32[512,16,512]{2,0,1:T(8,128)} %fusion.103, f32[16,512]{1,0:T(8,128)S(1)} %multiply_reduce_fusion.5, ...), kind=kOutput, calls=%fused_computation.25.clone.1 | convolution fusion | flops 6464471040 | bytes 21269008 | tf_op jit(solution)/shard_map/cond/branch_0_fun/while/body/eval_jaxpr/tjs,jsw->tw/dot_general | solution.py:14
  397.5 110.7 %all-reduce.2.cloned.1.call-done = f32[6144,128]{1,0:T(8,128)} async-done(((f32[6144,128]{1,0:T(8,128)}), f32[6144,128]{1,0:T(8,128)}) %all-reduce.2.cloned.1.call-update) | async-done | bytes 3145744 | tf_op jit(solution)/shard_map/psum | solution.py:91
  508.3 3.8 copy.79
  (72 shorter events, 31.7 us)
Async XLA Ops:
  6.5 24.8 %copy-start = (f32[6144,128]{1,0:T(8,128)S(1)}, f32[6144,128]{1,0:T(8,128)}, u32[]{:S(2)}) copy-start(f32[6144,128]{1,0:T(8,128)} %param.16) | copy-start | bytes 9437188
  8.0 11.9 %all-to-all-start = ((s32[8,1,2]{2,1,0:T(1,128)}), s32[8,1,2]{2,1,0:T(1,128)S(1)}, u32[]{:S(2)}, u32[]{:S(2)}) async-start(s32[8,1,2]{2,1,0:T(1,128)} %copy.24), calls=%async_computation | async-start | bytes 8192 | tf_op jit(solution)/shard_map/all_to_all | solution.py:32
  27.0 53.4 %all-to-all-start.1 = ((f32[8,2,64,512]{3,2,1,0:T(8,128)}), f32[8,2,64,512]{3,2,1,0:T(8,128)}, u32[]{:S(2)}, u32[]{:S(2)}) async-start(f32[8,2,64,512]{3,2,1,0:T(8,128)} %broadcast_select_fusion.1), calls=%async_computation.1 | async-start | bytes 4194304 | tf_op jit(solution)/shard_map/all_to_all | solution.py:35
  80.4 116.0 %all-to-all-start.2 = ((f32[8,2,512,128]{3,2,1,0:T(8,128)}), f32[8,2,512,128]{3,2,1,0:T(8,128)}, u32[]{:S(2)}, u32[]{:S(2)}) async-start(f32[8,2,512,128]{3,2,1,0:T(8,128)} %broadcast_select_fusion), calls=%async_computation.2 | async-start | bytes 8388608 | tf_op jit(solution)/shard_map/all_to_all | solution.py:36
  85.0 111.5 %all-gather.3.cloned.1.call-start = ((), (), s32[]{:S(2)}) async-start(), calls=%async_computation.4 | async-start | bytes 1179648 | tf_op jit(solution)/shard_map/all_gather | solution.py:57
  87.8 14.5 %copy-start.3 = (f32[64,6144]{1,0:T(8,128)S(1)}, f32[64,6144]{1,0:T(8,128)}, u32[]{:S(2)}) copy-start(f32[64,6144]{1,0:T(8,128)} %param.15) | copy-start | bytes 4718596
  87.9 5.8 %collective-permute-start = (f32[256,128]{1,0:T(8,128)S(1)}, f32[256,128]{1,0:T(8,128)S(1)}, u32[]{:S(2)}, u32[]{:S(2)}) collective-permute-start(f32[256,128]{1,0:T(8,128)S(1)} %fusion.70), channel_id=1, source_target_pairs={{0,8},{8,0},{16,24},{24,16},{1,9},{9,1},{17,25},{25,17},{2,10},{10... | collective-permute-start | bytes 393224 | tf_op jit(solution)/shard_map/ppermute | solution.py:52
  93.7 5.0 collective-permute-start.1
  99.4 5.2 %copy-start.5 = (s32[1,256]{1,0:T(1,128)S(1)}, s32[1,256]{1,0:T(1,128)}, u32[]{:S(2)}) copy-start(s32[1,256]{1,0:T(1,128)} %param.21) | copy-start | bytes 3076
  99.4 97.0 %copy-start.4 = (s32[12,8]{0,1:T(8,128)S(1)}, s32[12,8]{0,1:T(8,128)}, u32[]{:S(2)}) copy-start(s32[12,8]{0,1:T(8,128)} %param.20) | copy-start | bytes 1156
  99.4 408.8 %all-reduce.2.cloned.1.call-start = ((), (), s32[]{:S(2)}) async-start(), calls=%async_computation.3 | async-start | bytes 6291456 | tf_op jit(solution)/shard_map/psum | solution.py:91
  397.5 114.5 %copy-start.1 = (f32[6144,128]{1,0:T(8,128)S(1)}, f32[6144,128]{1,0:T(8,128)}, u32[]{:S(2)}) copy-start(f32[6144,128]{1,0:T(8,128)} %param.16) | copy-start | bytes 9437188
Sparse Core Ops, SparseCore 0:
  99.5 31.7 all-gather.2
  397.6 110.5 all-reduce.1
